TPU v7x, 32 devices: a whole 2x2x4 slice. The times are simulated.
32 devices in a mesh: ex: 2 (over core), ey: 16 (over z, y, x).
Axes of the slice: x: 2, y: 2, z: 4, core: 2. Of those that a mesh axis runs over, the one named last changes fastest.
Arguments:
- tokens: bfloat16 [32, 256, 1024], P(('ex', 'ey')), may hold values from -16 to 16
- slot_param: bfloat16 [1024, 32], replicated, may hold values from -0.75 to 0.75
- weight_in: bfloat16 [32, 1024, 4096], P('ey', None, 'ex'), may hold values from -0.1875 to 0.1875
- weight_out: bfloat16 [32, 4096, 1024], P('ey', 'ex'), may hold values from -0.09375 to 0.09375
- grad_out: bfloat16 [32, 256, 1024], P(('ex', 'ey')), may hold values from -6 to 6
Outputs:
- grad_tokens: bfloat16 [32, 256, 1024], P(('ex', 'ey'))
- grad_param: float32 [1024, 32], replicated
- grad_win: bfloat16 [32, 1024, 4096], P('ey', None, 'ex')
- grad_wout: bfloat16 [32, 4096, 1024], P('ey', 'ex')
All inputs are finite; a program needn't handle non-finite values.
Results may differ from a plain program's by a relative error of at most 0.017.
Values may be sent and summed in bfloat16 or wider, within the bound.
No kernel may reach another device: no remote copies, remote signals or barrier semaphores. Data moves between devices by JAX's collectives and lax.ppermute only.
A program may use at most 64 MiB of HBM per device.

v0:
```python
import jax
import jax.numpy as jnp
from jax import lax
from jax.sharding import PartitionSpec as P


def gelu_parts(pre):
    cdf = 0.5 * (1.0 + lax.erf(pre * 0.7071067811865476))
    slope = cdf + pre * jnp.exp(-0.5 * pre * pre) * 0.3989422804014327
    return (pre * cdf, slope)


def softmax_along(values, axis):
    top = jnp.max(values, axis=axis, keepdims=True)
    expo = jnp.exp(values - top)
    return expo / jnp.sum(expo, axis=axis, keepdims=True)


def route_in(stacked):
    moved = lax.all_to_all(stacked, "ey", split_axis=2, concat_axis=0, tiled=True)
    return lax.all_gather(moved, "ex", axis=0, tiled=True)


def route_out(term_fn, total_rows):
    summed = lax.psum_scatter(
        term_fn(jnp.int32(0), total_rows // lax.axis_size("ex") * lax.axis_size("ex")).astype(
            jnp.bfloat16
        ),
        "ex",
        scatter_dimension=0,
        tiled=True,
    )
    return lax.all_to_all(summed, "ey", split_axis=0, concat_axis=2, tiled=True)


def per_device(tokens, slot_param, weight_in, weight_out, grad_out):
    logits = jnp.einsum("ipd,ds->ips", tokens, slot_param, preferred_element_type=jnp.float32)
    dispatch = softmax_along(logits, 1)
    combine = softmax_along(logits, 2)
    dispatch_b = dispatch.astype(jnp.bfloat16)
    combine_b = combine.astype(jnp.bfloat16)
    slot_in = jnp.einsum(
        "ips,ipd->isd", dispatch_b, tokens, preferred_element_type=jnp.float32
    ).astype(jnp.bfloat16)
    slot_cot = jnp.einsum(
        "ips,ipd->isd", combine_b, grad_out, preferred_element_type=jnp.float32
    ).astype(jnp.bfloat16)
    arrived = route_in(jnp.stack((slot_in, slot_cot), axis=1))
    total_rows = arrived.shape[0]
    slot_x = arrived[:, 0]
    slot_g = arrived[:, 1]
    pre = jnp.einsum("red,edf->ref", slot_x, weight_in, preferred_element_type=jnp.float32)
    value, slope = gelu_parts(pre)
    hidden = value.astype(jnp.bfloat16)
    back = jnp.einsum("red,efd->ref", slot_g, weight_out, preferred_element_type=jnp.float32)
    dpre = (back * slope).astype(jnp.bfloat16)

    def paired_term(start, count):
        return jnp.concatenate(
            (
                jnp.einsum("ref,efd->red", hidden, weight_out, preferred_element_type=jnp.float32)[
                    :, None
                ],
                jnp.einsum("ref,edf->red", dpre, weight_in, preferred_element_type=jnp.float32)[
                    :, None
                ],
            ),
            axis=1,
        )

    paired = route_out(paired_term, total_rows)
    slot_out = paired[:, 0]
    grad_slot = paired[:, 1]
    grad_win = jnp.einsum("red,ref->edf", slot_x, dpre, preferred_element_type=jnp.float32).astype(
        jnp.bfloat16
    )
    grad_wout = jnp.einsum(
        "ref,red->efd", hidden, slot_g, preferred_element_type=jnp.float32
    ).astype(jnp.bfloat16)
    d_combine = jnp.einsum("ipd,isd->ips", grad_out, slot_out, preferred_element_type=jnp.float32)
    d_dispatch = jnp.einsum("ipd,isd->ips", tokens, grad_slot, preferred_element_type=jnp.float32)
    d_logits = dispatch * (d_dispatch - jnp.sum(dispatch * d_dispatch, axis=1, keepdims=True))
    d_logits = d_logits + combine * (
        d_combine - jnp.sum(combine * d_combine, axis=2, keepdims=True)
    )
    logit_grad = d_logits.astype(jnp.bfloat16)
    grad_tokens = jnp.einsum(
        "ips,isd->ipd", dispatch_b, grad_slot, preferred_element_type=jnp.float32
    )
    grad_tokens = grad_tokens + jnp.einsum(
        "ips,ds->ipd", logit_grad, slot_param, preferred_element_type=jnp.float32
    )
    local_param = jnp.einsum("ipd,ips->ds", tokens, logit_grad, preferred_element_type=jnp.float32)
    grad_param = lax.psum(local_param, ("ex", "ey"))
    return (grad_tokens.astype(jnp.bfloat16), grad_param, grad_win, grad_wout)


def solution(mesh):
    in_specs = (
        P(("ex", "ey"), None, None),
        P(),
        P("ey", None, "ex"),
        P("ey", "ex", None),
        P(("ex", "ey"), None, None),
    )
    out_specs = (P(("ex", "ey"), None, None), P(), P("ey", None, "ex"), P("ey", "ex", None))
    return jax.shard_map(
        per_device, mesh=mesh, in_specs=in_specs, out_specs=out_specs, check_vma=False
    )
```

profile of v0, /device:TPU:0, one launch (start us, length us, event | category | flops | bytes accessed | tf_op | source)
XLA Modules:
  0.0 198.2 jit_solution(10697608207090606354)
XLA Ops:
  7.2 0.0 copy-start
  7.2 0.0 reduce-scatter.2.cloned.1.call-start
  7.2 1.0 copy-done
  8.2 1.2 fusion.36
  9.4 0.2 fusion.25
  9.6 0.2 fusion.6
  9.9 1.2 fusion.7
  11.1 0.1 copy.17
  11.3 15.9 %all_to_all.36 = bf16[1,2,32,1024]{3,1,0,2:T(2,128)(2,1)S(1)} all-to-all(bf16[1,2,32,1024]{3,1,0,2:T(2,128)(2,1)S(1)} %copy.17), channel_id=1, replica_groups=mesh['ex'=2,'ey'=16] {'ey'}, dimensions={2} | all-to-all | bytes 262144 | tf_op jit(solution)/shard_map/all_to_all | solution.py:20
  27.2 0.0 slice-start
  27.3 2.1 %all-gather = bf16[32,1,2,2,1024]{4,0,3,2,1:T(8,128)(2,1)S(1)} all-gather(bf16[16,1,2,2,1024]{4,0,3,2,1:T(8,128)(2,1)S(1)} %bitcast.90), channel_id=2, replica_groups=mesh['ex'=2,'ey'=16] {'ex'}, dimensions={0}, use_global_device_ids=true | all-gather | bytes 393216 | tf_op jit(solution)/shard_map/all_gather | solution.py:21
  29.4 0.0 slice-start.1
  29.4 0.0 slice-start.2
  29.4 5.1 %convolution_bitcast_fusion.1 = f32[32,2,2048]{2,0,1:T(8,128)S(1)} fusion(bf16[2,1024,2048]{2,1,0:T(8,128)(2,1)} %param.7, bf16[32,2,2,1024]{3,0,2,1:T(8,128)(2,1)S(1)} %bitcast.85), kind=kOutput, calls=%fused_computation.4 | convolution fusion | flops 268435456 | bytes 9043968 | tf_op jit(solution)/shard_map/red,edf->ref/dot_general | solution.py:52
  34.5 0.0 slice-done
  34.5 0.0 slice-done.1
  34.5 0.0 slice-start.3
  34.5 1.5 fusion.4
  36.0 2.6 %fusion.1 = bf16[32,2,2048]{2,0,1:T(8,128)(2,1)S(1)} fusion(bf16[2,2048,1024]{2,1,0:T(8,128)(2,1)S(1)} %bitcast.82, f32[32,2,2048]{2,0,1:T(8,128)S(1)} %convolution_bitcast_fusion.1, bf16[32,2,2,1024]{3,0,2,1:T(8,128)(2,1)S(1)} %bitcast.86), kind=kOutput, calls=%fused_computation.5 | convolution fusion | flops 269746176 | bytes 9306112 | tf_op jit(solution)/shard_map/red,efd->ref/dot_general | solution.py:55
  38.6 0.0 slice-done.2
  38.7 0.0 slice-done.3
  38.7 2.6 %fusion.5 = bf16[32,1,2,1024]{3,0,2,1:T(8,128)(2,1)S(1)} fusion(bf16[32,2,2048]{2,0,1:T(8,128)(2,1)S(1)} %fusion.1, bf16[2,1024,2048]{2,1,0:T(8,128)(2,1)S(1)} %bitcast.84), kind=kOutput, calls=%fused_computation.12 | convolution fusion | flops 268500992 | bytes 8781824 | tf_op jit(solution)/shard_map/ref,edf->red/dot_general | solution.py:64
  41.2 0.7 pad_maximum_fusion
  42.0 0.0 reduce-scatter.2.cloned.1.call-update
  42.0 0.0 copy-start.1
  42.0 5.8 %convolution_convert_fusion = bf16[2,2048,1024]{2,1,0:T(8,128)(2,1)} fusion(bf16[32,2,2,1024]{3,0,2,1:T(8,128)(2,1)S(1)} %bitcast.87, f32[32,2,2048]{2,0,1:T(8,128)S(1)} %convolution_bitcast_fusion.1), kind=kOutput, calls=%fused_computation | convolution fusion | flops 273285120 | bytes 9043968 | tf_op jit(solution)/shard_map/ref,red->efd/dot_general | solution.py:77
  47.8 0.0 copy-start.2
  47.8 0.0 reduce-scatter.2.cloned.1.call-done
  47.8 1.7 copy.19
  49.5 6.0 %all-to-all-start.1 = ((bf16[16,2,2,1024]{3,2,1,0:T(2,128)(2,1)}), bf16[16,2,2,1024]{3,2,1,0:T(2,128)(2,1)S(1)}, u32[]{:S(2)}, u32[]{:S(2)}) async-start(bf16[16,2,2,1024]{3,2,1,0:T(2,128)(2,1)} %copy.19), calls=%async_computation.2 | async-start | bytes 262144 | tf_op jit(solution)/shard_map/all_to_all | solution.py:33
  55.5 0.2 all-reduce.2.cloned.1.call-start
  55.8 5.8 %convolution_convert_fusion.1 = bf16[2,1024,2048]{2,1,0:T(8,128)(2,1)} fusion(bf16[32,2,2048]{2,0,1:T(8,128)(2,1)S(1)} %fusion.1, bf16[32,2,2,1024]{3,0,2,1:T(8,128)(2,1)S(1)} %bitcast.88), kind=kOutput, calls=%fused_computation.1 | convolution fusion | flops 272629760 | bytes 8781824 | tf_op jit(solution)/shard_map/red,ref->edf/dot_general | solution.py:74
  61.6 1.9 all-to-all-done.1
  63.5 0.1 copy.20
  63.6 0.2 fusion.37
  63.8 0.0 copy-done.1
  63.8 0.3 convolution_bitcast_fusion.3
  64.1 0.4 fusion.22
  64.5 0.4 multiply_reduce_fusion.1
  64.8 0.9 convolution_bitcast_fusion.2
  65.8 0.0 all-reduce.2.cloned.1.call-update
  65.8 0.0 copy-done.2
  65.8 1.2 fusion.3
  67.0 122.8 %all-reduce.2.cloned.1.call-done = f32[1024,32]{0,1:T(8,128)} async-done(((f32[1024,32]{0,1:T(8,128)}), f32[1024,32]{0,1:T(8,128)}) %all-reduce.2.cloned.1.call-update) | async-done | bytes 131088 | tf_op jit(solution)/shard_map/psum | solution.py:94
  189.8 1.6 copy.40
  (4 shorter events, 0.1 us)
Async XLA Ops:
  7.2 1.0 copy-start
  7.2 40.6 %reduce-scatter.2.cloned.1.call-start = ((), (), s32[]{:S(2)}) async-start(), calls=%async_computation.3 | async-start | bytes 393216 | tf_op jit(solution)/shard_map/reduce_scatter | solution.py:25
  27.2 7.3 %slice-start = ((s8[8388608]{0:T(1024)(128)(4,1)}), s8[4194304]{0:T(1024)(128)(4,1)S(1)}, s32[]{:S(2)}) async-start(s8[8388608]{0:T(1024)(128)(4,1)} %bitcast.81), calls=%async_computation.5 | async-start | bytes 8388608
  29.4 5.1 %slice-start.1 = ((s8[8388608]{0:T(1024)(128)(4,1)}), s8[4194304]{0:T(1024)(128)(4,1)S(1)}, s32[]{:S(2)}) async-start(s8[8388608]{0:T(1024)(128)(4,1)} %bitcast.81), calls=%async_computation.6 | async-start | bytes 8388608
  29.4 9.3 %slice-start.2 = ((s8[8388608]{0:T(1024)(128)(4,1)}), s8[4194304]{0:T(1024)(128)(4,1)S(1)}, s32[]{:S(2)}) async-start(s8[8388608]{0:T(1024)(128)(4,1)} %bitcast.83), calls=%async_computation.7 | async-start | bytes 8388608
  34.5 4.2 %slice-start.3 = ((s8[8388608]{0:T(1024)(128)(4,1)}), s8[4194304]{0:T(1024)(128)(4,1)S(1)}, s32[]{:S(2)}) async-start(s8[8388608]{0:T(1024)(128)(4,1)} %bitcast.83), calls=%async_computation.8 | async-start | bytes 8388608
  42.0 21.8 %copy-start.1 = (bf16[1,256,1024]{2,1,0:T(8,128)(2,1)S(1)}, bf16[1,256,1024]{2,1,0:T(8,128)(2,1)}, u32[]{:S(2)}) copy-start(bf16[1,256,1024]{2,1,0:T(8,128)(2,1)} %param.9) | copy-start | bytes 1572868
  47.8 18.0 %copy-start.2 = (bf16[1024,32]{0,1:T(8,128)(2,1)S(1)}, bf16[1024,32]{0,1:T(8,128)(2,1)}, u32[]{:S(2)}) copy-start(bf16[1024,32]{0,1:T(8,128)(2,1)} %param.6) | copy-start | bytes 196612
  49.5 13.9 %all-to-all-start.1 = ((bf16[16,2,2,1024]{3,2,1,0:T(2,128)(2,1)}), bf16[16,2,2,1024]{3,2,1,0:T(2,128)(2,1)S(1)}, u32[]{:S(2)}, u32[]{:S(2)}) async-start(bf16[16,2,2,1024]{3,2,1,0:T(2,128)(2,1)} %copy.19), calls=%async_computation.2 | async-start | bytes 262144 | tf_op jit(solution)/shard_map/all_to_all | solution.py:33
  55.5 134.3 %all-reduce.2.cloned.1.call-start = ((), (), s32[]{:S(2)}) async-start(), calls=%async_computation.4 | async-start | bytes 262144 | tf_op jit(solution)/shard_map/psum | solution.py:94
Sparse Core Ops, SparseCore 0:
  42.1 4.9 reduce-scatter.1
  65.9 123.8 all-reduce.1
where the time goes:
time: 199 us; the launch traced here: 198 us
  waiting for transfers between devices  125 us (63%)
  matrix products  29.2 us (15%)
  blocking collectives  18.1 us (9%)
  between operations  14.2 us (7%)
  starting transfers between devices  6.26 us (3%)
  local copies, waits for them, and re-layouts  4.79 us (2%)
    psum x1, waiting for transfers between devices, per_device(): grad_param = lax.psum(local_param, ('ex', 'ey'))  123 us
    all_to_all x1, blocking collectives, route_in(): lax.all_to_all(stacked, 'ey', split_axis=2, concat_axis=0, tiled=True)  15.9 us
    all_to_all x1, starting transfers between devices, route_out(): return lax.all_to_all(summed, 'ey', split_axis=0, concat_axis=2, tiled=True)  6 us
    dot_general x1, matrix products, per_device(): jnp.einsum('ref,red->efd', hidden, slot_g, preferred_element_type=jnp.flo...  5.78 us
    dot_general x1, matrix products, per_device(): jnp.einsum('red,ref->edf', slot_x, dpre, preferred_element_type=jnp.float32)  5.78 us
    dot_general x1, matrix products, per_device(): jnp.einsum('red,edf->ref', slot_x, weight_in, preferred_element_type=jnp....  5.07 us
  transfers between devices with their start and end apart: 3, of which 2 were waited for; matrix products, arithmetic and copies ran while one was open for 6% of the time, Pallas kernels for 0%

commit v1 on v0

--- a/solution.py
+++ b/solution.py
@@ -91,7 +91,7 @@
         "ips,ds->ipd", logit_grad, slot_param, preferred_element_type=jnp.float32
     )
     local_param = jnp.einsum("ipd,ips->ds", tokens, logit_grad, preferred_element_type=jnp.float32)
-    grad_param = lax.psum(local_param, ("ex", "ey"))
+    grad_param = lax.psum(lax.psum(local_param, "ey"), "ex")
     return (grad_tokens.astype(jnp.bfloat16), grad_param, grad_win, grad_wout)
 
 

time: 199 us -> 198 us (level)
    psum x1 -> x2, waiting for transfers between devices: 123 us -> 123 us  [per_device(): grad_param = lax.psum(lax.psum(local_param, 'ey'), 'ex')]
  transfers between devices with their start and end apart: 3 -> 4, of which waited for: 2 -> 3; matrix products, arithmetic and copies ran while one was open for 6% -> 7% of each run, Pallas kernels for 0% -> 0%
where the time goes in v1:
time: 198 us
  waiting for transfers between devices  125 us (63%)
  matrix products  29.2 us (15%)
  blocking collectives  18.1 us (9%)
  between operations  13.9 us (7%)
  starting transfers between devices  6.3 us (3%)
  local copies, waits for them, and re-layouts  4.79 us (2%)
    psum x2, waiting for transfers between devices, per_device(): grad_param = lax.psum(lax.psum(local_param, 'ey'), 'ex')  123 us
    all_to_all x1, blocking collectives, route_in(): lax.all_to_all(stacked, 'ey', split_axis=2, concat_axis=0, tiled=True)  15.9 us
    all_to_all x1, starting transfers between devices, route_out(): return lax.all_to_all(summed, 'ey', split_axis=0, concat_axis=2, tiled=True)  6 us
    dot_general x1, matrix products, per_device(): jnp.einsum('ref,red->efd', hidden, slot_g, preferred_element_type=jnp.flo...  5.78 us
    dot_general x1, matrix products, per_device(): jnp.einsum('red,ref->edf', slot_x, dpre, preferred_element_type=jnp.float32)  5.78 us
    dot_general x1, matrix products, per_device(): jnp.einsum('red,edf->ref', slot_x, weight_in, preferred_element_type=jnp....  5.07 us
  transfers between devices with their start and end apart: 4, of which 3 were waited for; matrix products, arithmetic and copies ran while one was open for 7% of the time, Pallas kernels for 0%

profile of v1, /device:TPU:0, one launch (start us, length us, event | category | flops | bytes accessed | tf_op | source)
XLA Modules:
  0.0 197.8 jit_solution(2432095978926402383)
XLA Ops:
  7.2 0.0 copy-start
  7.2 0.0 reduce-scatter.2.cloned.1.call-start
  7.2 1.0 copy-done
  8.2 1.2 fusion.36
  9.4 0.2 fusion.25
  9.6 0.2 fusion.6
  9.9 1.2 fusion.7
  11.1 0.1 copy.17
  11.3 15.9 %all_to_all.36 = bf16[1,2,32,1024]{3,1,0,2:T(2,128)(2,1)S(1)} all-to-all(bf16[1,2,32,1024]{3,1,0,2:T(2,128)(2,1)S(1)} %copy.17), channel_id=1, replica_groups=mesh['ex'=2,'ey'=16] {'ey'}, dimensions={2} | all-to-all | bytes 262144 | tf_op jit(solution)/shard_map/all_to_all | solution.py:20
  27.2 0.0 slice-start
  27.3 2.1 %all-gather = bf16[32,1,2,2,1024]{4,0,3,2,1:T(8,128)(2,1)S(1)} all-gather(bf16[16,1,2,2,1024]{4,0,3,2,1:T(8,128)(2,1)S(1)} %bitcast.90), channel_id=2, replica_groups=mesh['ex'=2,'ey'=16] {'ex'}, dimensions={0}, use_global_device_ids=true | all-gather | bytes 393216 | tf_op jit(solution)/shard_map/all_gather | solution.py:21
  29.4 0.0 slice-start.1
  29.4 0.0 slice-start.2
  29.4 5.1 %convolution_bitcast_fusion.1 = f32[32,2,2048]{2,0,1:T(8,128)S(1)} fusion(bf16[2,1024,2048]{2,1,0:T(8,128)(2,1)} %param.7, bf16[32,2,2,1024]{3,0,2,1:T(8,128)(2,1)S(1)} %bitcast.85), kind=kOutput, calls=%fused_computation.4 | convolution fusion | flops 268435456 | bytes 9043968 | tf_op jit(solution)/shard_map/red,edf->ref/dot_general | solution.py:52
  34.5 0.0 slice-done
  34.5 0.0 slice-done.1
  34.5 0.0 slice-start.3
  34.5 1.5 fusion.4
  36.0 2.6 %fusion.1 = bf16[32,2,2048]{2,0,1:T(8,128)(2,1)S(1)} fusion(bf16[2,2048,1024]{2,1,0:T(8,128)(2,1)S(1)} %bitcast.82, f32[32,2,2048]{2,0,1:T(8,128)S(1)} %convolution_bitcast_fusion.1, bf16[32,2,2,1024]{3,0,2,1:T(8,128)(2,1)S(1)} %bitcast.86), kind=kOutput, calls=%fused_computation.5 | convolution fusion | flops 269746176 | bytes 9306112 | tf_op jit(solution)/shard_map/red,efd->ref/dot_general | solution.py:55
  38.6 0.0 slice-done.2
  38.7 0.0 slice-done.3
  38.7 2.6 %fusion.5 = bf16[32,1,2,1024]{3,0,2,1:T(8,128)(2,1)S(1)} fusion(bf16[32,2,2048]{2,0,1:T(8,128)(2,1)S(1)} %fusion.1, bf16[2,1024,2048]{2,1,0:T(8,128)(2,1)S(1)} %bitcast.84), kind=kOutput, calls=%fused_computation.12 | convolution fusion | flops 268500992 | bytes 8781824 | tf_op jit(solution)/shard_map/ref,edf->red/dot_general | solution.py:64
  41.2 0.7 pad_maximum_fusion
  42.0 0.0 reduce-scatter.2.cloned.1.call-update
  42.0 0.0 copy-start.1
  42.0 5.8 %convolution_convert_fusion = bf16[2,2048,1024]{2,1,0:T(8,128)(2,1)} fusion(bf16[32,2,2,1024]{3,0,2,1:T(8,128)(2,1)S(1)} %bitcast.87, f32[32,2,2048]{2,0,1:T(8,128)S(1)} %convolution_bitcast_fusion.1), kind=kOutput, calls=%fused_computation | convolution fusion | flops 273285120 | bytes 9043968 | tf_op jit(solution)/shard_map/ref,red->efd/dot_general | solution.py:77
  47.8 0.0 copy-start.2
  47.8 0.0 reduce-scatter.2.cloned.1.call-done
  47.8 1.7 copy.19
  49.5 6.0 %all-to-all-start.1 = ((bf16[16,2,2,1024]{3,2,1,0:T(2,128)(2,1)}), bf16[16,2,2,1024]{3,2,1,0:T(2,128)(2,1)S(1)}, u32[]{:S(2)}, u32[]{:S(2)}) async-start(bf16[16,2,2,1024]{3,2,1,0:T(2,128)(2,1)} %copy.19), calls=%async_computation.2 | async-start | bytes 262144 | tf_op jit(solution)/shard_map/all_to_all | solution.py:33
  55.5 0.2 all-reduce.3.cloned.1.call-start
  55.8 5.8 %convolution_convert_fusion.1 = bf16[2,1024,2048]{2,1,0:T(8,128)(2,1)} fusion(bf16[32,2,2048]{2,0,1:T(8,128)(2,1)S(1)} %fusion.1, bf16[32,2,2,1024]{3,0,2,1:T(8,128)(2,1)S(1)} %bitcast.88), kind=kOutput, calls=%fused_computation.1 | convolution fusion | flops 272629760 | bytes 8781824 | tf_op jit(solution)/shard_map/red,ref->edf/dot_general | solution.py:74
  61.6 1.9 all-to-all-done.1
  63.5 0.1 copy.20
  63.6 0.2 fusion.37
  63.8 0.0 copy-done.1
  63.8 0.3 convolution_bitcast_fusion.3
  64.1 0.4 multiply_reduce_fusion.1
  64.4 0.9 convolution_bitcast_fusion.2
  65.4 0.0 all-reduce.3.cloned.1.call-update
  65.4 0.0 all-reduce.5.cloned.1.call-start
  65.4 0.4 fusion.22
  65.8 104.5 %all-reduce.3.cloned.1.call-done = f32[1024,32]{0,1:T(8,128)} async-done(((f32[1024,32]{0,1:T(8,128)}), f32[1024,32]{0,1:T(8,128)}) %all-reduce.3.cloned.1.call-update) | async-done | bytes 131088 | tf_op jit(solution)/shard_map/psum | solution.py:94
  170.4 0.0 all-reduce.5.cloned.1.call-update
  170.4 0.0 copy-done.2
  170.4 1.2 fusion.3
  171.6 18.1 %all-reduce.5.cloned.1.call-done = f32[1024,32]{0,1:T(8,128)} async-done(((f32[1024,32]{0,1:T(8,128)}), f32[1024,32]{0,1:T(8,128)}) %all-reduce.5.cloned.1.call-update) | async-done | bytes 131088 | tf_op jit(solution)/shard_map/psum | solution.py:94
  189.7 1.6 copy.41
  (4 shorter events, 0.1 us)
Async XLA Ops:
  7.2 1.0 copy-start
  7.2 40.6 %reduce-scatter.2.cloned.1.call-start = ((), (), s32[]{:S(2)}) async-start(), calls=%async_computation.3 | async-start | bytes 393216 | tf_op jit(solution)/shard_map/reduce_scatter | solution.py:25
  27.2 7.3 %slice-start = ((s8[8388608]{0:T(1024)(128)(4,1)}), s8[4194304]{0:T(1024)(128)(4,1)S(1)}, s32[]{:S(2)}) async-start(s8[8388608]{0:T(1024)(128)(4,1)} %bitcast.81), calls=%async_computation.6 | async-start | bytes 8388608
  29.4 5.1 %slice-start.1 = ((s8[8388608]{0:T(1024)(128)(4,1)}), s8[4194304]{0:T(1024)(128)(4,1)S(1)}, s32[]{:S(2)}) async-start(s8[8388608]{0:T(1024)(128)(4,1)} %bitcast.81), calls=%async_computation.7 | async-start | bytes 8388608
  29.4 9.3 %slice-start.2 = ((s8[8388608]{0:T(1024)(128)(4,1)}), s8[4194304]{0:T(1024)(128)(4,1)S(1)}, s32[]{:S(2)}) async-start(s8[8388608]{0:T(1024)(128)(4,1)} %bitcast.83), calls=%async_computation.8 | async-start | bytes 8388608
  34.5 4.2 %slice-start.3 = ((s8[8388608]{0:T(1024)(128)(4,1)}), s8[4194304]{0:T(1024)(128)(4,1)S(1)}, s32[]{:S(2)}) async-start(s8[8388608]{0:T(1024)(128)(4,1)} %bitcast.83), calls=%async_computation.9 | async-start | bytes 8388608
  42.0 21.8 %copy-start.1 = (bf16[1,256,1024]{2,1,0:T(8,128)(2,1)S(1)}, bf16[1,256,1024]{2,1,0:T(8,128)(2,1)}, u32[]{:S(2)}) copy-start(bf16[1,256,1024]{2,1,0:T(8,128)(2,1)} %param.9) | copy-start | bytes 1572868
  47.8 122.6 %copy-start.2 = (bf16[1024,32]{0,1:T(8,128)(2,1)S(1)}, bf16[1024,32]{0,1:T(8,128)(2,1)}, u32[]{:S(2)}) copy-start(bf16[1024,32]{0,1:T(8,128)(2,1)} %param.6) | copy-start | bytes 196612
  49.5 13.9 %all-to-all-start.1 = ((bf16[16,2,2,1024]{3,2,1,0:T(2,128)(2,1)}), bf16[16,2,2,1024]{3,2,1,0:T(2,128)(2,1)S(1)}, u32[]{:S(2)}, u32[]{:S(2)}) async-start(bf16[16,2,2,1024]{3,2,1,0:T(2,128)(2,1)} %copy.19), calls=%async_computation.2 | async-start | bytes 262144 | tf_op jit(solution)/shard_map/all_to_all | solution.py:33
  55.5 114.8 %all-reduce.3.cloned.1.call-start = ((), (), s32[]{:S(2)}) async-start(), calls=%async_computation.4 | async-start | bytes 262144 | tf_op jit(solution)/shard_map/psum | solution.py:94
  65.4 124.3 %all-reduce.5.cloned.1.call-start = ((), (), s32[]{:S(2)}) async-start(), calls=%async_computation.5 | async-start | bytes 262144 | tf_op jit(solution)/shard_map/psum | solution.py:94
Sparse Core Ops, SparseCore 0:
  42.1 4.9 reduce-scatter.1
  65.5 104.8 all-reduce.2
  172.7 16.9 all-reduce.4
